TPU v7x, 32 devices: a whole 2x2x4 slice. The times are simulated.
32 devices in a mesh: section: 4 (over y, core), shard: 2 (over x), tensor: 4 (over z).
Axes of the slice: x: 2, y: 2, z: 4, core: 2. Of those that a mesh axis runs over, the one named last changes fastest.
Arguments:
- gradient: bfloat16 [48, 2560, 1024], P('section', ('shard', 'tensor')), may hold values from -15000 to 15000
- momentum: float32 [48, 2560, 1024], P('section', ('shard', 'tensor')), may hold values from -28000 to 28000
- weight: bfloat16 [48, 2560, 1024], P('section', ('shard', 'tensor')), may hold values from -0.1875 to 0.1875
Outputs:
- new_weight: bfloat16 [48, 2560, 1024], P('section', ('shard', 'tensor'))
- new_momentum: float32 [48, 2560, 1024], P('section', ('shard', 'tensor'))
- update: bfloat16 [48, 2560, 1024], P('section', ('shard', 'tensor'))
All inputs are finite; a program needn't handle non-finite values.
Results may differ from a plain program's by a relative error of at most 0.029.
Values may be sent and summed in bfloat16 or wider, within the bound.
A program may use at most 256 MiB of HBM per device.

v0:
```python
import math

import jax
import jax.numpy as jnp
from jax import lax
from jax.sharding import PartitionSpec as P

D = 1024
HID = 2560
ITERS = 3


decay_rate = 0.95
epsilon = 1e-07
coeff_one = 3.4445
coeff_two = -4.775
coeff_three = 2.0315
learn_rate = 0.02
weight_decay = 0.1


def shortened(x):

    def short(part):
        return part.astype(jnp.bfloat16) if part.dtype == jnp.float32 else part

    return jax.tree.map(short, x)


def gram_matrix(partial_value):
    return lax.psum(partial_value.astype(jnp.bfloat16), "tensor").astype(jnp.float32)


def orthogonalize(nesterov):
    values = nesterov.astype(jnp.float32)
    total = lax.psum(jnp.sum(values * values, axis=(1, 2)), "tensor")
    current = (values / (jnp.sqrt(total)[:, None, None] + epsilon)).astype(jnp.bfloat16)
    for iteration in range(ITERS):
        partial_value = jnp.einsum(
            "krd,kre->kde", current, current, preferred_element_type=jnp.float32
        )
        gram = gram_matrix(partial_value)
        gram_bf = gram.astype(jnp.bfloat16)
        squared = jnp.einsum("kde,kef->kdf", gram_bf, gram_bf, preferred_element_type=jnp.float32)
        mixer = (coeff_two * gram + coeff_three * squared).astype(jnp.bfloat16)
        mixed = jnp.einsum("krd,kde->kre", current, mixer, preferred_element_type=jnp.float32)
        current = (coeff_one * current.astype(jnp.float32) + mixed).astype(jnp.bfloat16)
    update_gain = 0.2 * math.sqrt(max(HID, D))
    return (update_gain * current.astype(jnp.float32)).astype(jnp.bfloat16)


def apply_update(weight, update):
    weight_values = weight.astype(jnp.float32)
    return (
        weight_values - learn_rate * (update.astype(jnp.float32) + weight_decay * weight_values)
    ).astype(jnp.bfloat16)


def pad_slots(values, padded_count):
    extra = padded_count - values.shape[0]
    if extra == 0:
        return values
    filler = jnp.zeros((extra,) + values.shape[1:], values.dtype)
    return jnp.concatenate([values, filler], axis=0)


def local(gradient, momentum, weight):
    section_mats = gradient.shape[0]
    shards = lax.axis_size("shard")
    slot_count = (section_mats + shards - 1) // shards
    padded_count = slot_count * shards
    grad_dealt, weight_dealt = (
        lax.all_to_all(
            pad_slots(gradient, padded_count), "shard", split_axis=0, concat_axis=1, tiled=True
        ),
        lax.all_to_all(
            pad_slots(weight, padded_count), "shard", split_axis=0, concat_axis=1, tiled=True
        ),
    )
    moment_dealt = lax.all_to_all(
        pad_slots(momentum, padded_count).astype(jnp.bfloat16),
        "shard",
        split_axis=0,
        concat_axis=1,
        tiled=True,
    ).astype(jnp.float32)
    grad_values = grad_dealt.astype(jnp.float32)
    new_momentum = decay_rate * moment_dealt + grad_values
    nesterov = (grad_values + decay_rate * new_momentum).astype(jnp.bfloat16)
    update = orthogonalize(nesterov)
    new_weight = apply_update(weight_dealt, update)
    back_weight, back_update = (
        lax.all_to_all(new_weight, "shard", split_axis=1, concat_axis=0, tiled=True),
        lax.all_to_all(update, "shard", split_axis=1, concat_axis=0, tiled=True),
    )
    back_moment = lax.all_to_all(
        shortened(new_momentum), "shard", split_axis=1, concat_axis=0, tiled=True
    ).astype(new_momentum.dtype)
    return (back_weight[:section_mats], back_moment[:section_mats], back_update[:section_mats])


def solution(mesh):
    return jax.shard_map(
        local,
        mesh=mesh,
        in_specs=(
            P("section", ("shard", "tensor"), None),
            P("section", ("shard", "tensor"), None),
            P("section", ("shard", "tensor"), None),
        ),
        out_specs=(
            P("section", ("shard", "tensor"), None),
            P("section", ("shard", "tensor"), None),
            P("section", ("shard", "tensor"), None),
        ),
        check_vma=False,
    )
```

profile of v0, /device:TPU:0, one launch (start us, length us, event | category | flops | bytes accessed | tf_op | source)
XLA Modules:
  0.0 1968.6 jit_solution(14599514388412769811)
XLA Ops:
  17.1 98.9 %all_to_all.72 = bf16[12,320,1024]{2,1,0:T(8,128)(2,1)} all-to-all(bf16[12,320,1024]{2,1,0:T(8,128)(2,1)} %convert_element_type.139), channel_id=1, replica_groups=mesh['section'=4,'shard'=2,'tensor'=4] {'shard'}, dimensions={0} | all-to-all | bytes 15728640 | tf_op jit(solution)/shard_map/all_to_all | solution.py:80
  134.2 14.5 copy.17
  148.6 60.6 %all-to-all-done.1 = bf16[12,320,1024]{2,1,0:T(8,128)(2,1)} async-done(((bf16[12,320,1024]{2,1,0:T(8,128)(2,1)}), bf16[12,320,1024]{2,1,0:T(8,128)(2,1)}, u32[]{:S(2)}, u32[]{:S(2)}) %all-to-all-start.1) | async-done | bytes 7864352 | tf_op jit(solution)/shard_map/all_to_all | solution.py:73
  229.5 12.4 psum.28
  241.9 16.3 fusion.22
  258.1 17.3 convolution_convert_fusion.2
  275.7 423.3 %all-reduce.4.cloned.1.call-done = bf16[6,1024,1024]{2,1,0:T(8,128)(2,1)} async-done(((bf16[6,1024,1024]{2,1,0:T(8,128)(2,1)}), bf16[6,1024,1024]{2,1,0:T(8,128)(2,1)}) %all-reduce.4.cloned.1.call-update) | async-done | bytes 12582928 | tf_op jit(solution)/shard_map/psum | solution.py:31
  699.0 35.4 %add_convert_fusion.5 = bf16[6,640,1024]{2,1,0:T(8,128)(2,1)} fusion(bf16[6,640,1024]{2,1,0:T(8,128)(2,1)} %get-tuple-element.4, bf16[6,1024,1024]{2,1,0:T(8,128)(2,1)} %all-reduce.4.cloned.1.call-done), kind=kOutput, calls=%fused_computation.19 | convolution fusion | flops 20985151488 | bytes 28311552 | tf_op jit(solution)/shard_map/krd,kde->kre/dot_general | solution.py:46
  734.4 17.3 convolution_convert_fusion.1
  752.0 424.9 %all-reduce.6.cloned.1.call-done = bf16[6,1024,1024]{2,1,0:T(8,128)(2,1)} async-done(((bf16[6,1024,1024]{2,1,0:T(8,128)(2,1)}), bf16[6,1024,1024]{2,1,0:T(8,128)(2,1)}) %all-reduce.6.cloned.1.call-update) | async-done | bytes 12582928 | tf_op jit(solution)/shard_map/psum | solution.py:31
  1176.9 35.2 %add_convert_fusion.4 = bf16[6,640,1024]{2,1,0:T(8,128)(2,1)} fusion(bf16[6,640,1024]{2,1,0:T(8,128)(2,1)} %add_convert_fusion.5, bf16[6,1024,1024]{2,1,0:T(8,128)(2,1)} %all-reduce.6.cloned.1.call-done), kind=kOutput, calls=%fused_computation.18 | convolution fusion | flops 20985151488 | bytes 28311552 | tf_op jit(solution)/shard_map/krd,kde->kre/dot_general | solution.py:46
  1212.1 17.2 convolution_convert_fusion
  1229.3 91.9 %all_to_all.73 = bf16[12,320,1024]{2,1,0:T(8,128)(2,1)S(1)} all-to-all(bf16[12,320,1024]{2,1,0:T(8,128)(2,1)} %param.5), channel_id=1, replica_groups=mesh['section'=4,'shard'=2,'tensor'=4] {'shard'}, dimensions={0} | all-to-all | bytes 15728640 | tf_op jit(solution)/shard_map/all_to_all | solution.py:76
  1329.1 12.1 copy.23
  1349.0 305.5 %all-reduce.8.cloned.1.call-done = bf16[6,1024,1024]{2,1,0:T(8,128)(2,1)} async-done(((bf16[6,1024,1024]{2,1,0:T(8,128)(2,1)}), bf16[6,1024,1024]{2,1,0:T(8,128)(2,1)}) %all-reduce.8.cloned.1.call-update) | async-done | bytes 12582928 | tf_op jit(solution)/shard_map/psum | solution.py:31
  1654.5 38.6 %fusion.2 = (bf16[6,640,1024]{2,1,0:T(8,128)(2,1)}, bf16[6,640,1024]{2,1,0:T(8,128)(2,1)}) fusion(f32[2,6,320,1024]{3,2,0,1:T(8,128)} %copy.15, bf16[6,640,1024]{2,1,0:T(8,128)(2,1)} %add_convert_fusion.4, bf16[6,1024,1024]{2,1,0:T(8,128)(2,1)} %all-reduce.8.cloned.1.call-done), kind=kOutput, calls=%fused_computation.9 | convolution fusion | flops 21020540928 | bytes 51904512 | tf_op jit(solution)/shard_map/krd,kde->kre/dot_general | solution.py:46
  1693.2 12.0 copy.21
  1713.1 11.8 copy.25
  1725.0 103.2 %all-to-all-done.3 = bf16[6,640,1024]{2,0,1:T(8,128)(2,1)} async-done(((bf16[6,640,1024]{2,0,1:T(8,128)(2,1)}), bf16[6,640,1024]{2,0,1:T(8,128)(2,1)}, u32[]{:S(2)}, u32[]{:S(2)}) %all-to-all-start.3) | async-done | bytes 7864352 | tf_op jit(solution)/shard_map/all_to_all | solution.py:93
  1835.8 13.9 convert_bitcast_fusion
  1849.7 17.9 copy.24
  1867.6 11.6 copy.22
  1879.2 70.8 %all-to-all-done.5 = bf16[6,640,1024]{2,0,1:T(8,128)(2,1)} async-done(((bf16[6,640,1024]{2,0,1:T(8,128)(2,1)}), bf16[6,640,1024]{2,0,1:T(8,128)(2,1)}, u32[]{:S(2)}, u32[]{:S(2)}) %all-to-all-start.5) | async-done | bytes 7864352 | tf_op jit(solution)/shard_map/all_to_all | solution.py:94
  1950.0 11.6 copy.26
  (17 shorter events, 80.1 us)
Async XLA Ops:
  116.0 93.2 %all-to-all-start.1 = ((bf16[12,320,1024]{2,1,0:T(8,128)(2,1)}), bf16[12,320,1024]{2,1,0:T(8,128)(2,1)}, u32[]{:S(2)}, u32[]{:S(2)}) async-start(bf16[12,320,1024]{2,1,0:T(8,128)(2,1)} %param.3), calls=%async_computation.1 | async-start | bytes 15728640 | tf_op jit(solution)/shard_map/all_to_all | solution.py:73
  122.8 576.2 %all-reduce.4.cloned.1.call-start = ((), (), s32[]{:S(2)}) async-start(), calls=%async_computation.6 | async-start | bytes 25165824 | tf_op jit(solution)/shard_map/psum | solution.py:31
  275.4 901.5 %all-reduce.6.cloned.1.call-start = ((), (), s32[]{:S(2)}) async-start(), calls=%async_computation.7 | async-start | bytes 25165824 | tf_op jit(solution)/shard_map/psum | solution.py:31
  751.8 902.8 %all-reduce.8.cloned.1.call-start = ((), (), s32[]{:S(2)}) async-start(), calls=%async_computation.8 | async-start | bytes 25165824 | tf_op jit(solution)/shard_map/psum | solution.py:31
  1341.2 364.0 %all-to-all-start.4 = ((bf16[6,640,1024]{2,0,1:T(8,128)(2,1)}), bf16[6,640,1024]{2,0,1:T(8,128)(2,1)}, u32[]{:S(2)}, u32[]{:S(2)}) async-start(bf16[6,640,1024]{2,0,1:T(8,128)(2,1)} %copy.23), calls=%async_computation.4 | async-start | bytes 20971520 | tf_op jit(solution)/shard_map/all_to_all | solution.py:96
  1705.2 123.0 %all-to-all-start.3 = ((bf16[6,640,1024]{2,0,1:T(8,128)(2,1)}), bf16[6,640,1024]{2,0,1:T(8,128)(2,1)}, u32[]{:S(2)}, u32[]{:S(2)}) async-start(bf16[6,640,1024]{2,0,1:T(8,128)(2,1)} %copy.21), calls=%async_computation.3 | async-start | bytes 20971520 | tf_op jit(solution)/shard_map/all_to_all | solution.py:93
  1828.2 121.9 %all-to-all-start.5 = ((bf16[6,640,1024]{2,0,1:T(8,128)(2,1)}), bf16[6,640,1024]{2,0,1:T(8,128)(2,1)}, u32[]{:S(2)}, u32[]{:S(2)}) async-start(bf16[6,640,1024]{2,0,1:T(8,128)(2,1)} %copy.25), calls=%async_computation.5 | async-start | bytes 20971520 | tf_op jit(solution)/shard_map/all_to_all | solution.py:94
Sparse Core Ops, SparseCore 0:
  275.6 423.3 all-reduce.3
  751.9 425.0 all-reduce.5
  1229.5 425.0 all-reduce.7
where the time goes:
time: 1980 us; the launch traced here: 1970 us
  waiting for transfers between devices  1390 us (70%)
  blocking collectives  203 us (10%)
  matrix products  161 us (8%)
  local copies, waits for them, and re-layouts  110 us (6%)
  other arithmetic  60.6 us (3%)
  starting transfers between devices  30.7 us (2%)
    psum x3, waiting for transfers between devices, gram_matrix(): lax.psum(partial_value.astype(jnp.bfloat16), 'tensor').astype(jnp.float32)  1150 us
    dot_general x3, matrix products, orthogonalize(): jnp.einsum('krd,kde->kre', current, mixer, preferred_element_type=jnp.flo...  109 us
    all_to_all x1, waiting for transfers between devices, local(): lax.all_to_all(new_weight, 'shard', split_axis=1, concat_axis=0, tiled=True)  103 us
    all_to_all x1, blocking collectives, local(): lax.all_to_all(pad_slots(momentum, padded_count).astype(jnp.bfloat16), 's...  98.9 us
    all_to_all x1, blocking collectives, local(): lax.all_to_all(pad_slots(weight, padded_count), 'shard', split_axis=0, co...  91.9 us
    all_to_all x1, waiting for transfers between devices, local(): lax.all_to_all(update, 'shard', split_axis=1, concat_axis=0, tiled=True)  70.8 us
    all_to_all x1, waiting for transfers between devices, local(): lax.all_to_all(pad_slots(gradient, padded_count), 'shard', split_axis=0,...  60.6 us
    dot_general x3, matrix products, orthogonalize(): jnp.einsum('krd,kre->kde', current, current, preferred_element_type=jnp.f...  51.8 us
  transfers between devices with their start and end apart: 7, of which 6 were waited for; matrix products, arithmetic and copies ran while one was open for 8% of the time, Pallas kernels for 0%

commit v1 on v0

v1 whole, which is shorter than its diff:
```python
import math

import jax
import jax.numpy as jnp
from jax import lax
from jax.experimental import pallas as pl
from jax.experimental.pallas import tpu as pltpu
from jax.sharding import PartitionSpec as P

ITERS = 3
BLK = 256
CHUNK = 1

decay_rate = 0.95
epsilon = 1e-07
coeff_one = 3.4445
coeff_two = -4.775
coeff_three = 2.0315
learn_rate = 0.02
weight_decay = 0.1


def pieces(width):
    nb = width // BLK
    half = BLK // 2
    out = []
    for i in range(nb):
        for j in range(i, nb):
            for h in range(2):
                if i == 0:
                    row, col = h * half, j * BLK
                elif 2 * i < nb:
                    row, col = i * BLK + h * half, (j - i) * BLK
                elif 2 * i > nb:
                    row, col = (nb - i) * BLK + h * half, j * BLK
                else:
                    row, col = i * BLK, (j - i) * BLK + h * (width // 2)
                out.append((i, j, h, row, col))
    return out


def packed_rows(width):
    return (width // BLK // 2) * BLK + BLK // 2


def gram_kernel(*refs):
    inputs, out_ref = refs[:-1], refs[-1]
    width = out_ref.shape[2]
    nb = width // BLK
    half = BLK // 2
    contract = (((0,), (0,)), ((), ()))
    for i in range(nb):
        value = None
        for ref in inputs:
            term = lax.dot_general(
                ref[0, :, pl.ds(i * BLK, BLK)],
                ref[0, :, pl.ds(i * BLK, width - i * BLK)],
                contract,
                preferred_element_type=jnp.float32,
            )
            value = term if value is None else value + term
        value = value.astype(jnp.bfloat16)
        for bi, bj, h, row, col in pieces(width):
            if bi == i:
                out_ref[0, pl.ds(row, half), pl.ds(col, BLK)] = value[
                    h * half : (h + 1) * half, (bj - i) * BLK : (bj - i + 1) * BLK
                ]


def gram_packed(*inputs):
    count, width = inputs[0].shape[0], inputs[0].shape[2]
    rows = packed_rows(width)
    depth = sum(x.shape[1] for x in inputs)
    return pl.pallas_call(
        gram_kernel,
        grid=(count,),
        in_specs=[pl.BlockSpec((1,) + x.shape[1:], lambda k: (k, 0, 0)) for x in inputs],
        out_specs=pl.BlockSpec((1, rows, width), lambda k: (k, 0, 0)),
        out_shape=jax.ShapeDtypeStruct((count, rows, width), jnp.bfloat16),
        compiler_params=pltpu.CompilerParams(vmem_limit_bytes=32 << 20),
        cost_estimate=pl.CostEstimate(
            flops=count * 2 * depth * width**2,
            bytes_accessed=count * 2 * (depth + rows) * width,
            transcendentals=0,
        ),
    )(*inputs)


def newton_kernel(gain, packed_ref, inputs, outputs, gram, total, gram_b, mix_b, total_b, holder):
    width = gram.shape[0]
    nb = width // BLK
    half = BLK // 2

    def blk(i):
        return pl.ds(i * BLK, BLK)

    trace = jnp.zeros((1, 1), jnp.float32)
    row_id = lax.broadcasted_iota(jnp.int32, (half, BLK), 0)
    col_id = lax.broadcasted_iota(jnp.int32, (half, BLK), 1)
    for i, j, h, row, col in pieces(width):
        if i == j:
            part = packed_ref[0, pl.ds(row, half), pl.ds(col, BLK)].astype(jnp.float32)
            part = jnp.where(row_id + h * half == col_id, part, 0.0)
            trace = trace + jnp.sum(jnp.sum(part, axis=1, keepdims=True), axis=0, keepdims=True)
    inverse = 1.0 / (jnp.sqrt(trace) + epsilon)
    for i, j, h, row, col in pieces(width):
        part = packed_ref[0, pl.ds(row, half), pl.ds(col, BLK)].astype(jnp.float32)
        gram[pl.ds(i * BLK + h * half, half), blk(j)] = part * inverse * inverse
    for i in range(nb):
        for j in range(i, nb):
            value = gram[blk(i), blk(j)]
            gram_b[blk(i), blk(j)] = value.astype(jnp.bfloat16)
            if j > i:
                gram_b[blk(j), blk(i)] = value.T.astype(jnp.bfloat16)

    def product(left, right, finish, full=None, keep=None):
        for i in range(nb):
            cols = pl.ds(i * BLK, width - i * BLK)
            value = jnp.dot(left[blk(i), :], right[:, cols], preferred_element_type=jnp.float32)
            value = finish(blk(i), cols, value)
            if keep is not None:
                keep[blk(i), cols] = value
            if full is not None:
                full[blk(i), cols] = value.astype(jnp.bfloat16)
                for j in range(i + 1, nb):
                    part = value[:, (j - i) * BLK : (j - i + 1) * BLK]
                    full[blk(j), blk(i)] = part.T.astype(jnp.bfloat16)

    def step_of(step, lead):
        product(
            gram_b,
            gram_b,
            lambda r, c, v: coeff_two * gram[r, c] + coeff_three * v,
            full=mix_b,
        )

        @pl.when(step == 0)
        def _():
            for i in range(nb):
                cols = pl.ds(i * BLK, width - i * BLK)
                total[blk(i), cols] = mix_b[blk(i), cols].astype(jnp.float32)
            total_b[...] = mix_b[...]

        @pl.when(step > 0)
        def _():
            def join(r, c, v):
                return coeff_one * total[r, c] + lead * mix_b[r, c].astype(jnp.float32) + v

            product(total_b, mix_b, join, keep=total, full=holder)
            total_b[...] = holder[...]

        @pl.when(step < ITERS - 1)
        def _():
            product(
                gram_b,
                mix_b,
                lambda r, c, v: coeff_one * gram[r, c] + v,
                full=holder,
                keep=gram,
            )
            product(
                mix_b,
                holder,
                lambda r, c, v: coeff_one * gram[r, c] + v,
                full=gram_b,
                keep=gram,
            )

        return lead * coeff_one

    lax.fori_loop(0, ITERS, step_of, jnp.float32(1.0))
    scale = inverse * gain
    for i in range(nb):
        for j in range(i, nb):
            value = total[blk(i), blk(j)]
            if i == j:
                r = lax.broadcasted_iota(jnp.int32, (BLK, BLK), 0)
                c = lax.broadcasted_iota(jnp.int32, (BLK, BLK), 1)
                value = value + jnp.where(r == c, coeff_one**ITERS, 0.0)
            value = value * scale
            holder[blk(i), blk(j)] = value.astype(jnp.bfloat16)
            if j > i:
                holder[blk(j), blk(i)] = value.T.astype(jnp.bfloat16)


    for x, out in zip(inputs, outputs):
        out[0] = jnp.dot(x[0], holder[...], preferred_element_type=jnp.float32).astype(
            jnp.bfloat16
        )


def updates(packed, gain, *inputs):
    count, rows, width = packed.shape
    parts = len(inputs)
    depth = sum(x.shape[1] for x in inputs)

    def kernel(packed_ref, *refs):
        newton_kernel(gain, packed_ref, refs[:parts], refs[parts : 2 * parts], *refs[2 * parts :])

    specs = [pl.BlockSpec((1,) + x.shape[1:], lambda k: (k, 0, 0)) for x in inputs]
    return pl.pallas_call(
        kernel,
        grid=(count,),
        in_specs=[pl.BlockSpec((1, rows, width), lambda k: (k, 0, 0))] + specs,
        out_specs=specs,
        out_shape=[jax.ShapeDtypeStruct(x.shape, jnp.bfloat16) for x in inputs],
        scratch_shapes=[pltpu.VMEM((width, width), jnp.float32)] * 2
        + [pltpu.VMEM((width, width), jnp.bfloat16)] * 4,
        compiler_params=pltpu.CompilerParams(vmem_limit_bytes=48 << 20),
        cost_estimate=pl.CostEstimate(
            flops=count * (12 * width**3 + 2 * depth * width**2),
            bytes_accessed=count * (2 * rows + 4 * depth) * width,
            transcendentals=0,
        ),
    )(packed, *inputs)


def gram_sum(packed):
    if lax.axis_size("tensor") != 4:
        return lax.psum(packed, "tensor")

    def added(x, y):
        return (x.astype(jnp.float32) + y.astype(jnp.float32)).astype(jnp.bfloat16)

    place = lax.axis_index("tensor")
    inner = added(packed, lax.ppermute(packed, "tensor", [(0, 1), (3, 2)]))
    whole = added(inner, lax.ppermute(inner, "tensor", [(1, 2), (2, 1)]))
    handed = lax.ppermute(whole, "tensor", [(1, 0), (2, 3)])
    return jnp.where((place == 1) | (place == 2), whole, handed)


def pad_slots(values, padded_count):
    extra = padded_count - values.shape[0]
    if extra == 0:
        return values
    filler = jnp.zeros((extra,) + values.shape[1:], values.dtype)
    return jnp.concatenate([values, filler], axis=0)


def update_pairs(nesterov, gain):
    half = nesterov.shape[0] // 2
    me = lax.axis_index("shard")
    swap = [(0, 1), (1, 0)]
    own, back = [], []
    for start in range(0, half, CHUNK):
        size = min(CHUNK, half - start)
        kept = lax.dynamic_slice_in_dim(nesterov, me * half + start, size, 0)
        sent = lax.dynamic_slice_in_dim(nesterov, (1 - me) * half + start, size, 0)
        got = lax.ppermute(sent, "shard", swap)
        packed = gram_sum(gram_packed(kept, got))
        mine, theirs = updates(packed, gain, kept, got)
        back.append(lax.ppermute(theirs, "shard", swap))
        own.append(mine)
    first = jnp.concatenate(own + back, axis=0)
    second = jnp.concatenate(back + own, axis=0)
    return jnp.where(me == 0, first, second)


def update_dealt(nesterov, shards, gain):
    count = nesterov.shape[0]
    slots = (count + shards - 1) // shards
    dealt = lax.all_to_all(
        pad_slots(nesterov, slots * shards), "shard", split_axis=0, concat_axis=1, tiled=True
    )
    (turned,) = updates(gram_sum(gram_packed(dealt)), gain, dealt)
    update = lax.all_to_all(turned, "shard", split_axis=1, concat_axis=0, tiled=True)
    return update[:count]


def local(gradient, momentum, weight):
    shards = lax.axis_size("shard")
    hidden = gradient.shape[1] * shards * lax.axis_size("tensor")
    gain = 0.2 * math.sqrt(max(hidden, gradient.shape[2]))
    grad_values = gradient.astype(jnp.float32)
    new_momentum = decay_rate * momentum + grad_values
    nesterov = (grad_values + decay_rate * new_momentum).astype(jnp.bfloat16)
    if shards == 2 and gradient.shape[0] % 2 == 0:
        update = update_pairs(nesterov, gain)
    else:
        update = update_dealt(nesterov, shards, gain)
    weight_values = weight.astype(jnp.float32)
    new_weight = (
        weight_values - learn_rate * (update.astype(jnp.float32) + weight_decay * weight_values)
    ).astype(jnp.bfloat16)
    return (new_weight, new_momentum, update)


def solution(mesh):
    spec = P("section", ("shard", "tensor"), None)
    return jax.shard_map(
        local,
        mesh=mesh,
        in_specs=(spec, spec, spec),
        out_specs=(spec, spec, spec),
        check_vma=False,
    )
```

time: 1980 us -> 480 us (0.24)
  waiting for transfers between devices: 1390 us -> 237 us
  blocking collectives: 203 us -> 0 us
  matrix products: 161 us -> 0 us
  Pallas kernels: 0 us -> 119 us
  local copies, waits for them, and re-layouts: 110 us -> 15.3 us
  starting transfers between devices: 30.7 us -> 53 us
    psum x3 -> x0, waiting for transfers between devices: 1150 us -> none  [gram_matrix(): lax.psum(partial_value.astype(jnp.bfloat16), 'tensor').astype(jnp.float32)]
    ppermute x0 -> x30, waiting for transfers between devices: none -> 237 us  [the longest x6 89.7 us: gram_sum(): handed = lax.ppermute(whole, 'tensor', [(1, 0), (2, 3)])]
    all_to_all x4 -> x0, waiting for transfers between devices: 235 us -> none  [the longest x1 103 us: local(): lax.all_to_all(new_weight, 'shard', split_axis=1, concat_axis=0, tiled=True)]
    all_to_all x2 -> x0, blocking collectives: 191 us -> none  [the longest x1 98.9 us: local(): lax.all_to_all(pad_slots(momentum, padded_count).astype(jnp.bfloat16), 's...]
    dot_general x6 -> x0, matrix products: 161 us -> none  [the longest x3 109 us: orthogonalize(): jnp.einsum('krd,kde->kre', current, mixer, preferred_element_type=jnp.flo...]
    pallas_call x0 -> x12, Pallas kernels: none -> 119 us  [the longest x6 109 us: updates(): pl.pallas_call(kernel, grid=(count,), in_specs=[pl.BlockSpec((1, rows, wi...]
    convert_element_type x6 -> x0, local copies, waits for them, and re-layouts: 72.7 us -> none  [the longest x1 17.9 us: local(): back_moment = lax.all_to_all(shortened(new_momentum), 'shard', split_axis...]
    ppermute x0 -> x30, starting transfers between devices: none -> 53 us  [the longest x6 21.7 us: gram_sum(): inner = added(packed, lax.ppermute(packed, 'tensor', [(0, 1), (3, 2)]))]
  transfers between devices with their start and end apart: 7 -> 30, of which waited for: 6 -> 16; matrix products, arithmetic and copies ran while one was open for 8% -> 6% of each run, Pallas kernels for 0% -> 25%
where the time goes in v1:
time: 480 us; the launch traced here: 471 us
  waiting for transfers between devices  237 us (49%)
  Pallas kernels  119 us (25%)
  starting transfers between devices  53 us (11%)
  other arithmetic  45.9 us (10%)
  local copies, waits for them, and re-layouts  15.3 us (3%)
    pallas_call x6, Pallas kernels, updates(): pl.pallas_call(kernel, grid=(count,), in_specs=[pl.BlockSpec((1, rows, wi...  109 us
    ppermute x6, waiting for transfers between devices, gram_sum(): handed = lax.ppermute(whole, 'tensor', [(1, 0), (2, 3)])  89.7 us
    ppermute x6, waiting for transfers between devices, gram_sum(): inner = added(packed, lax.ppermute(packed, 'tensor', [(0, 1), (3, 2)]))  86.9 us
    ppermute x6, waiting for transfers between devices, update_pairs(): got = lax.ppermute(sent, 'shard', swap)  54.9 us
    ppermute x6, starting transfers between devices, gram_sum(): inner = added(packed, lax.ppermute(packed, 'tensor', [(0, 1), (3, 2)]))  21.7 us
    convert_element_type x12, other arithmetic, added(): return (x.astype(jnp.float32) + y.astype(jnp.float32)).astype(jnp.bfloat16)  18.6 us
    convert_element_type x1, other arithmetic, local(): nesterov = (grad_values + decay_rate * new_momentum).astype(jnp.bfloat16)  14.3 us
    unnamed x64, local copies, waits for them, and re-layouts  14.2 us
  transfers between devices with their start and end apart: 30, of which 16 were waited for; matrix products, arithmetic and copies ran while one was open for 6% of the time, Pallas kernels for 25%

profile of v1, /device:TPU:0, one launch (start us, length us, event | category | flops | bytes accessed | tf_op | source)
XLA Modules:
  0.0 471.1 jit_solution(13940882265989918944)
XLA Ops:
  0.6 14.3 %fusion.3 = (bf16[12,320,1024]{2,1,0:T(8,128)(2,1)S(1)}, f32[12,320,1024]{2,1,0:T(8,128)}) fusion(bf16[12,320,1024]{2,1,0:T(8,128)(2,1)} %param.3, f32[12,320,1024]{2,1,0:T(8,128)} %param.4), kind=kLoop, calls=%fused_computation.7 | loop fusion | flops 23592960 | bytes 47185920 | tf_op jit(solution)/shard_map/convert_element_type | solution.py:276
  21.0 13.5 %collective-permute-done.20.refs_1_ = bf16[1,320,1024]{2,1,0:T(8,128)(2,1)S(1)} collective-permute-done((bf16[1,320,1024]{2,1,0:T(8,128)(2,1)S(1)}, bf16[1,320,1024]{2,1,0:T(8,128)(2,1)S(1)}, u32[]{:S(2)}, u32[]{:S(2)}) %collective-permute-start.20) | collective-permute-done | bytes 655392 | tf_op jit(solution)/shard_map/ppermute | solution.py:249
  41.7 6.8 %collective-permute-done.16.refs_1_ = bf16[1,320,1024]{2,1,0:T(8,128)(2,1)S(1)} collective-permute-done((bf16[1,320,1024]{2,1,0:T(8,128)(2,1)S(1)}, bf16[1,320,1024]{2,1,0:T(8,128)(2,1)S(1)}, u32[]{:S(2)}, u32[]{:S(2)}) %collective-permute-start.16) | collective-permute-done | bytes 655392 | tf_op jit(solution)/shard_map/ppermute | solution.py:249
  54.2 8.3 %collective-permute-done.12.refs_1_ = bf16[1,320,1024]{2,1,0:T(8,128)(2,1)S(1)} collective-permute-done((bf16[1,320,1024]{2,1,0:T(8,128)(2,1)S(1)}, bf16[1,320,1024]{2,1,0:T(8,128)(2,1)S(1)}, u32[]{:S(2)}, u32[]{:S(2)}) %collective-permute-start.12) | collective-permute-done | bytes 655392 | tf_op jit(solution)/shard_map/ppermute | solution.py:249
  66.1 10.4 %collective-permute-done.8.refs_1_ = bf16[1,320,1024]{2,1,0:T(8,128)(2,1)S(1)} collective-permute-done((bf16[1,320,1024]{2,1,0:T(8,128)(2,1)S(1)}, bf16[1,320,1024]{2,1,0:T(8,128)(2,1)S(1)}, u32[]{:S(2)}, u32[]{:S(2)}) %collective-permute-start.8) | collective-permute-done | bytes 655392 | tf_op jit(solution)/shard_map/ppermute | solution.py:249
  82.2 8.4 %collective-permute-done.4.refs_1_ = bf16[1,320,1024]{2,1,0:T(8,128)(2,1)S(1)} collective-permute-done((bf16[1,320,1024]{2,1,0:T(8,128)(2,1)S(1)}, bf16[1,320,1024]{2,1,0:T(8,128)(2,1)S(1)}, u32[]{:S(2)}, u32[]{:S(2)}) %collective-permute-start.4) | collective-permute-done | bytes 655392 | tf_op jit(solution)/shard_map/ppermute | solution.py:249
  96.3 7.5 %collective-permute-done.refs_1_ = bf16[1,320,1024]{2,1,0:T(8,128)(2,1)S(1)} collective-permute-done((bf16[1,320,1024]{2,1,0:T(8,128)(2,1)S(1)}, bf16[1,320,1024]{2,1,0:T(8,128)(2,1)S(1)}, u32[]{:S(2)}, u32[]{:S(2)}) %collective-permute-start) | collective-permute-done | bytes 655392 | tf_op jit(solution)/shard_map/ppermute | solution.py:249
  112.4 13.0 %collective-permute-done.13 = bf16[1,640,1024]{2,1,0:T(8,128)(2,1)S(1)} collective-permute-done((bf16[1,640,1024]{2,1,0:T(8,128)(2,1)S(1)}, bf16[1,640,1024]{2,1,0:T(8,128)(2,1)S(1)}, u32[]{:S(2)}, u32[]{:S(2)}) %collective-permute-start.13) | collective-permute-done | bytes 1310752 | tf_op jit(solution)/shard_map/ppermute | solution.py:226
  126.9 26.6 %collective-permute-done.9 = bf16[1,640,1024]{2,1,0:T(8,128)(2,1)S(1)} collective-permute-done((bf16[1,640,1024]{2,1,0:T(8,128)(2,1)S(1)}, bf16[1,640,1024]{2,1,0:T(8,128)(2,1)S(1)}, u32[]{:S(2)}, u32[]{:S(2)}) %collective-permute-start.9) | collective-permute-done | bytes 1310752 | tf_op jit(solution)/shard_map/ppermute | solution.py:226
  155.9 25.7 %collective-permute-done.5 = bf16[1,640,1024]{2,1,0:T(8,128)(2,1)S(1)} collective-permute-done((bf16[1,640,1024]{2,1,0:T(8,128)(2,1)S(1)}, bf16[1,640,1024]{2,1,0:T(8,128)(2,1)S(1)}, u32[]{:S(2)}, u32[]{:S(2)}) %collective-permute-start.5) | collective-permute-done | bytes 1310752 | tf_op jit(solution)/shard_map/ppermute | solution.py:226
  184.9 21.6 %collective-permute-done.1 = bf16[1,640,1024]{2,1,0:T(8,128)(2,1)S(1)} collective-permute-done((bf16[1,640,1024]{2,1,0:T(8,128)(2,1)S(1)}, bf16[1,640,1024]{2,1,0:T(8,128)(2,1)S(1)}, u32[]{:S(2)}, u32[]{:S(2)}) %collective-permute-start.1) | collective-permute-done | bytes 1310752 | tf_op jit(solution)/shard_map/ppermute | solution.py:226
  231.4 17.9 %collective-permute-done.23 = bf16[1,640,1024]{2,1,0:T(8,128)(2,1)} collective-permute-done((bf16[1,640,1024]{2,1,0:T(8,128)(2,1)}, bf16[1,640,1024]{2,1,0:T(8,128)(2,1)}, u32[]{:S(2)}, u32[]{:S(2)}) %collective-permute-start.23) | collective-permute-done | bytes 1310752 | tf_op jit(solution)/shard_map/ppermute | solution.py:228
  250.8 26.6 %collective-permute-done.19 = bf16[1,640,1024]{2,1,0:T(8,128)(2,1)} collective-permute-done((bf16[1,640,1024]{2,1,0:T(8,128)(2,1)}, bf16[1,640,1024]{2,1,0:T(8,128)(2,1)}, u32[]{:S(2)}, u32[]{:S(2)}) %collective-permute-start.19) | collective-permute-done | bytes 1310752 | tf_op jit(solution)/shard_map/ppermute | solution.py:228
  279.3 18.2 %shard_map.67 = (bf16[1,320,1024]{2,1,0:T(8,128)(2,1)S(1)}, bf16[1,320,1024]{2,1,0:T(8,128)(2,1)}) custom-call(bf16[1,640,1024]{2,1,0:T(8,128)(2,1)S(1)} %get-tuple-element.56.packed_ref, bf16[1,320,1024]{2,1,0:T(8,128)(2,1)S(1)} %copy-done.1, bf16[1,320,1024]{2,1,0:T(8,128)(2,1)S(1)} %copy-done.17), custom_call_target="tpu_custom_call" | custom-call | flops 14227079168 | bytes 3932160 | tf_op jit(solution)/shard_map/pallas_call | solution.py:201
  299.0 6.5 %collective-permute-done.15 = bf16[1,640,1024]{2,1,0:T(8,128)(2,1)} collective-permute-done((bf16[1,640,1024]{2,1,0:T(8,128)(2,1)S(1)}, bf16[1,640,1024]{2,1,0:T(8,128)(2,1)}, u32[]{:S(2)}, u32[]{:S(2)}) %collective-permute-start.15) | collective-permute-done | bytes 1310752 | tf_op jit(solution)/shard_map/ppermute | solution.py:228
  305.4 28.1 %collective-permute-done.11 = bf16[1,640,1024]{2,1,0:T(8,128)(2,1)} collective-permute-done((bf16[1,640,1024]{2,1,0:T(8,128)(2,1)S(1)}, bf16[1,640,1024]{2,1,0:T(8,128)(2,1)}, u32[]{:S(2)}, u32[]{:S(2)}) %collective-permute-start.11) | collective-permute-done | bytes 1310752 | tf_op jit(solution)/shard_map/ppermute | solution.py:228
  335.5 18.4 %shard_map.63 = (bf16[1,320,1024]{2,1,0:T(8,128)(2,1)S(1)}, bf16[1,320,1024]{2,1,0:T(8,128)(2,1)}) custom-call(bf16[1,640,1024]{2,1,0:T(8,128)(2,1)S(1)} %get-tuple-element.58.packed_ref, bf16[1,320,1024]{2,1,0:T(8,128)(2,1)S(1)} %get-tuple-element.38.refs_0_, bf16[1,320,1024]{2,1,0:T(8,128)(2,1)S(1)} %copy-done.15), custom_call_target="tpu_custom_call" | custom-call | flops 14227079168 | bytes 3932160 | tf_op jit(solution)/shard_map/pallas_call | solution.py:201
  355.4 18.6 %shard_map.65 = (bf16[1,320,1024]{2,1,0:T(8,128)(2,1)S(1)}, bf16[1,320,1024]{2,1,0:T(8,128)(2,1)}) custom-call(bf16[1,640,1024]{2,1,0:T(8,128)(2,1)S(1)} %get-tuple-element.57.packed_ref, bf16[1,320,1024]{2,1,0:T(8,128)(2,1)S(1)} %get-tuple-element.36.refs_0_, bf16[1,320,1024]{2,1,0:T(8,128)(2,1)S(1)} %copy-done.11), custom_call_target="tpu_custom_call" | custom-call | flops 14227079168 | bytes 3932160 | tf_op jit(solution)/shard_map/pallas_call | solution.py:201
  374.6 10.7 %collective-permute-done.3 = bf16[1,640,1024]{2,1,0:T(8,128)(2,1)S(1)} collective-permute-done((bf16[1,640,1024]{2,1,0:T(8,128)(2,1)S(1)}, bf16[1,640,1024]{2,1,0:T(8,128)(2,1)S(1)}, u32[]{:S(2)}, u32[]{:S(2)}) %collective-permute-start.3) | collective-permute-done | bytes 1310752 | tf_op jit(solution)/shard_map/ppermute | solution.py:228
  385.6 17.5 %shard_map.59 = (bf16[1,320,1024]{2,1,0:T(8,128)(2,1)S(1)}, bf16[1,320,1024]{2,1,0:T(8,128)(2,1)S(1)}) custom-call(bf16[1,640,1024]{2,1,0:T(8,128)(2,1)S(1)} %get-tuple-element.60.packed_ref, bf16[1,320,1024]{2,1,0:T(8,128)(2,1)S(1)} %get-tuple-element.42.refs_0_, bf16[1,320,1024]{2,1,0:T(8,128)(2,1)S(1)} %copy-done.13), custom_call_target="tpu_custom_call" | custom-call | flops 14227079168 | bytes 3932160 | tf_op jit(solution)/shard_map/pallas_call | solution.py:201
  404.6 18.4 %shard_map.61 = (bf16[1,320,1024]{2,1,0:T(8,128)(2,1)S(1)}, bf16[1,320,1024]{2,1,0:T(8,128)(2,1)}) custom-call(bf16[1,640,1024]{2,1,0:T(8,128)(2,1)S(1)} %get-tuple-element.59.packed_ref, bf16[1,320,1024]{2,1,0:T(8,128)(2,1)S(1)} %get-tuple-element.40.refs_0_, bf16[1,320,1024]{2,1,0:T(8,128)(2,1)S(1)} %copy-done.9), custom_call_target="tpu_custom_call" | custom-call | flops 14227079168 | bytes 3932160 | tf_op jit(solution)/shard_map/pallas_call | solution.py:201
  423.5 18.4 %shard_map.69 = (bf16[1,320,1024]{2,1,0:T(8,128)(2,1)S(1)}, bf16[1,320,1024]{2,1,0:T(8,128)(2,1)}) custom-call(bf16[1,640,1024]{2,1,0:T(8,128)(2,1)S(1)} %get-tuple-element.55.packed_ref, bf16[1,320,1024]{2,1,0:T(8,128)(2,1)S(1)} %get-tuple-element.32.refs_0_, bf16[1,320,1024]{2,1,0:T(8,128)(2,1)S(1)} %copy-done.7), custom_call_target="tpu_custom_call" | custom-call | flops 14227079168 | bytes 3932160 | tf_op jit(solution)/shard_map/pallas_call | solution.py:201
  449.9 5.0 %collective-permute-done.29 = bf16[1,320,1024]{2,1,0:T(8,128)(2,1)S(1)} collective-permute-done((bf16[1,320,1024]{2,1,0:T(8,128)(2,1)}, bf16[1,320,1024]{2,1,0:T(8,128)(2,1)S(1)}, u32[]{:S(2)}, u32[]{:S(2)}) %collective-permute-start.29) | collective-permute-done | bytes 655392 | tf_op jit(solution)/shard_map/ppermute | solution.py:252
  461.8 8.8 %fusion.2 = (bf16[12,320,1024]{2,1,0:T(8,128)(2,1)}, bf16[12,320,1024]{2,1,0:T(8,128)(2,1)}) fusion(bf16[12,320,1024]{2,1,0:T(8,128)(2,1)S(1)} %bitcast.1, bf16[12,320,1024]{2,1,0:T(8,128)(2,1)S(1)} %constant_dynamic-update-slice_fusion, bf16[12,320,1024]{2,1,0:T(8,128)(2,1)S(1)} %get-tuple-element.43, pred[]{:T(512)S(6)} %eq.6), kind=kLoop, calls=%fused_computation.6 | loop fusion | flops 31457280 | bytes 39321600 | tf_op jit(solution)/shard_map/convert_element_type | solution.py:284
  (133 shorter events, 100.4 us)
Async XLA Ops:
  18.9 43.6 %collective-permute-start.12 = (bf16[1,320,1024]{2,1,0:T(8,128)(2,1)S(1)}, bf16[1,320,1024]{2,1,0:T(8,128)(2,1)S(1)}, u32[]{:S(2)}, u32[]{:S(2)}) collective-permute-start(bf16[1,320,1024]{2,1,0:T(8,128)(2,1)S(1)} %get-tuple-element.35), channel_id=1, source_target_pairs={{0,4},{4,0},{1,5},{5,1},{2,6},{6,2},{3,7},{7,3},{8,12},{12,8},{9,1... | collective-permute-start | bytes 1966088 | tf_op jit(solution)/shard_map/ppermute | solution.py:249
  20.9 55.7 %collective-permute-start.8 = (bf16[1,320,1024]{2,1,0:T(8,128)(2,1)S(1)}, bf16[1,320,1024]{2,1,0:T(8,128)(2,1)S(1)}, u32[]{:S(2)}, u32[]{:S(2)}) collective-permute-start(bf16[1,320,1024]{2,1,0:T(8,128)(2,1)S(1)} %get-tuple-element.37), channel_id=1, source_target_pairs={{0,4},{4,0},{1,5},{5,1},{2,6},{6,2},{3,7},{7,3},{8,12},{12,8},{9,1... | collective-permute-start | bytes 1966088 | tf_op jit(solution)/shard_map/ppermute | solution.py:249
  36.0 73.2 %collective-permute-start.21 = (bf16[1,640,1024]{2,1,0:T(8,128)(2,1)S(1)}, bf16[1,640,1024]{2,1,0:T(8,128)(2,1)S(1)}, u32[]{:S(2)}, u32[]{:S(2)}) collective-permute-start(bf16[1,640,1024]{2,1,0:T(8,128)(2,1)S(1)} %shard_map.68), channel_id=1, source_target_pairs={{0,1},{3,2},{4,5},{7,6},{8,9},{11,10},{12,13},{15,14},{16,17},{19,... | collective-permute-start | bytes 3932168 | tf_op jit(solution)/shard_map/ppermute | solution.py:226
  40.1 50.5 %collective-permute-start.4 = (bf16[1,320,1024]{2,1,0:T(8,128)(2,1)S(1)}, bf16[1,320,1024]{2,1,0:T(8,128)(2,1)S(1)}, u32[]{:S(2)}, u32[]{:S(2)}) collective-permute-start(bf16[1,320,1024]{2,1,0:T(8,128)(2,1)S(1)} %get-tuple-element.39), channel_id=1, source_target_pairs={{0,4},{4,0},{1,5},{5,1},{2,6},{6,2},{3,7},{7,3},{8,12},{12,8},{9,1... | collective-permute-start | bytes 1966088 | tf_op jit(solution)/shard_map/ppermute | solution.py:249
  50.0 61.1 %collective-permute-start.17 = (bf16[1,640,1024]{2,1,0:T(8,128)(2,1)S(1)}, bf16[1,640,1024]{2,1,0:T(8,128)(2,1)S(1)}, u32[]{:S(2)}, u32[]{:S(2)}) collective-permute-start(bf16[1,640,1024]{2,1,0:T(8,128)(2,1)S(1)} %shard_map.66), channel_id=1, source_target_pairs={{0,1},{3,2},{4,5},{7,6},{8,9},{11,10},{12,13},{15,14},{16,17},{19,... | collective-permute-start | bytes 3932168 | tf_op jit(solution)/shard_map/ppermute | solution.py:226
  62.5 41.3 %collective-permute-start = (bf16[1,320,1024]{2,1,0:T(8,128)(2,1)S(1)}, bf16[1,320,1024]{2,1,0:T(8,128)(2,1)S(1)}, u32[]{:S(2)}, u32[]{:S(2)}) collective-permute-start(bf16[1,320,1024]{2,1,0:T(8,128)(2,1)S(1)} %get-tuple-element.41), channel_id=1, source_target_pairs={{0,4},{4,0},{1,5},{5,1},{2,6},{6,2},{3,7},{7,3},{8,12},{12,8},{9,1... | collective-permute-start | bytes 1966088 | tf_op jit(solution)/shard_map/ppermute | solution.py:249
  76.6 48.9 %collective-permute-start.13 = (bf16[1,640,1024]{2,1,0:T(8,128)(2,1)S(1)}, bf16[1,640,1024]{2,1,0:T(8,128)(2,1)S(1)}, u32[]{:S(2)}, u32[]{:S(2)}) collective-permute-start(bf16[1,640,1024]{2,1,0:T(8,128)(2,1)S(1)} %shard_map.64), channel_id=1, source_target_pairs={{0,1},{3,2},{4,5},{7,6},{8,9},{11,10},{12,13},{15,14},{16,17},{19,... | collective-permute-start | bytes 3932168 | tf_op jit(solution)/shard_map/ppermute | solution.py:226
  90.6 62.9 %collective-permute-start.9 = (bf16[1,640,1024]{2,1,0:T(8,128)(2,1)S(1)}, bf16[1,640,1024]{2,1,0:T(8,128)(2,1)S(1)}, u32[]{:S(2)}, u32[]{:S(2)}) collective-permute-start(bf16[1,640,1024]{2,1,0:T(8,128)(2,1)S(1)} %shard_map.62), channel_id=1, source_target_pairs={{0,1},{3,2},{4,5},{7,6},{8,9},{11,10},{12,13},{15,14},{16,17},{19,... | collective-permute-start | bytes 3932168 | tf_op jit(solution)/shard_map/ppermute | solution.py:226
  103.8 77.8 %collective-permute-start.5 = (bf16[1,640,1024]{2,1,0:T(8,128)(2,1)S(1)}, bf16[1,640,1024]{2,1,0:T(8,128)(2,1)S(1)}, u32[]{:S(2)}, u32[]{:S(2)}) collective-permute-start(bf16[1,640,1024]{2,1,0:T(8,128)(2,1)S(1)} %shard_map.60), channel_id=1, source_target_pairs={{0,1},{3,2},{4,5},{7,6},{8,9},{11,10},{12,13},{15,14},{16,17},{19,... | collective-permute-start | bytes 3932168 | tf_op jit(solution)/shard_map/ppermute | solution.py:226
  109.2 97.3 %collective-permute-start.1 = (bf16[1,640,1024]{2,1,0:T(8,128)(2,1)S(1)}, bf16[1,640,1024]{2,1,0:T(8,128)(2,1)S(1)}, u32[]{:S(2)}, u32[]{:S(2)}) collective-permute-start(bf16[1,640,1024]{2,1,0:T(8,128)(2,1)S(1)} %shard_map.58), channel_id=1, source_target_pairs={{0,1},{3,2},{4,5},{7,6},{8,9},{11,10},{12,13},{15,14},{16,17},{19,... | collective-permute-start | bytes 3932168 | tf_op jit(solution)/shard_map/ppermute | solution.py:226
  111.1 98.7 %collective-permute-start.22 = (bf16[1,640,1024]{2,1,0:T(8,128)(2,1)S(1)}, bf16[1,640,1024]{2,1,0:T(8,128)(2,1)S(1)}, u32[]{:S(2)}, u32[]{:S(2)}) collective-permute-start(bf16[1,640,1024]{2,1,0:T(8,128)(2,1)S(1)} %add_convert_fusion.1), channel_id=1, source_target_pairs={{1,2},{2,1},{5,6},{6,5},{9,10},{10,9},{13,14},{14,13},{17,18},{18,... | collective-permute-start | bytes 3932168 | tf_op jit(solution)/shard_map/ppermute | solution.py:227
  125.4 87.7 %collective-permute-start.18 = (bf16[1,640,1024]{2,1,0:T(8,128)(2,1)S(1)}, bf16[1,640,1024]{2,1,0:T(8,128)(2,1)S(1)}, u32[]{:S(2)}, u32[]{:S(2)}) collective-permute-start(bf16[1,640,1024]{2,1,0:T(8,128)(2,1)S(1)} %add_convert_fusion.3), channel_id=1, source_target_pairs={{1,2},{2,1},{5,6},{6,5},{9,10},{10,9},{13,14},{14,13},{17,18},{18,... | collective-permute-start | bytes 3932168 | tf_op jit(solution)/shard_map/ppermute | solution.py:227
  153.5 62.5 %collective-permute-start.14 = (bf16[1,640,1024]{2,1,0:T(8,128)(2,1)S(1)}, bf16[1,640,1024]{2,1,0:T(8,128)(2,1)S(1)}, u32[]{:S(2)}, u32[]{:S(2)}) collective-permute-start(bf16[1,640,1024]{2,1,0:T(8,128)(2,1)S(1)} %add_convert_fusion.5), channel_id=1, source_target_pairs={{1,2},{2,1},{5,6},{6,5},{9,10},{10,9},{13,14},{14,13},{17,18},{18,... | collective-permute-start | bytes 3932168 | tf_op jit(solution)/shard_map/ppermute | solution.py:227
  181.6 39.1 %collective-permute-start.10 = (bf16[1,640,1024]{2,1,0:T(8,128)(2,1)}, bf16[1,640,1024]{2,1,0:T(8,128)(2,1)}, u32[]{:S(2)}, u32[]{:S(2)}) collective-permute-start(bf16[1,640,1024]{2,1,0:T(8,128)(2,1)} %add_convert_fusion.7), channel_id=1, source_target_pairs={{1,2},{2,1},{5,6},{6,5},{9,10},{10,9},{13,14},{14,13},{17,18},{18,... | collective-permute-start | bytes 3932168 | tf_op jit(solution)/shard_map/ppermute | solution.py:227
  213.1 36.1 %collective-permute-start.23 = (bf16[1,640,1024]{2,1,0:T(8,128)(2,1)}, bf16[1,640,1024]{2,1,0:T(8,128)(2,1)}, u32[]{:S(2)}, u32[]{:S(2)}) collective-permute-start(bf16[1,640,1024]{2,1,0:T(8,128)(2,1)} %add_convert_fusion), channel_id=1, source_target_pairs={{1,0},{2,3},{5,4},{6,7},{9,8},{10,11},{13,12},{14,15},{17,16},{18,... | collective-permute-start | bytes 3932168 | tf_op jit(solution)/shard_map/ppermute | solution.py:228
  217.1 60.2 %collective-permute-start.19 = (bf16[1,640,1024]{2,1,0:T(8,128)(2,1)}, bf16[1,640,1024]{2,1,0:T(8,128)(2,1)}, u32[]{:S(2)}, u32[]{:S(2)}) collective-permute-start(bf16[1,640,1024]{2,1,0:T(8,128)(2,1)} %add_convert_fusion.2), channel_id=1, source_target_pairs={{1,0},{2,3},{5,4},{6,7},{9,8},{10,11},{13,12},{14,15},{17,16},{18,... | collective-permute-start | bytes 3932168 | tf_op jit(solution)/shard_map/ppermute | solution.py:228
  220.7 84.8 %collective-permute-start.15 = (bf16[1,640,1024]{2,1,0:T(8,128)(2,1)S(1)}, bf16[1,640,1024]{2,1,0:T(8,128)(2,1)}, u32[]{:S(2)}, u32[]{:S(2)}) collective-permute-start(bf16[1,640,1024]{2,1,0:T(8,128)(2,1)S(1)} %add_convert_fusion.4), channel_id=1, source_target_pairs={{1,0},{2,3},{5,4},{6,7},{9,8},{10,11},{13,12},{14,15},{17,16},{18,... | collective-permute-start | bytes 3932168 | tf_op jit(solution)/shard_map/ppermute | solution.py:228
  224.2 109.3 %collective-permute-start.11 = (bf16[1,640,1024]{2,1,0:T(8,128)(2,1)S(1)}, bf16[1,640,1024]{2,1,0:T(8,128)(2,1)}, u32[]{:S(2)}, u32[]{:S(2)}) collective-permute-start(bf16[1,640,1024]{2,1,0:T(8,128)(2,1)S(1)} %add_convert_fusion.6), channel_id=1, source_target_pairs={{1,0},{2,3},{5,4},{6,7},{9,8},{10,11},{13,12},{14,15},{17,16},{18,... | collective-permute-start | bytes 3932168 | tf_op jit(solution)/shard_map/ppermute | solution.py:228
  227.8 146.8 %collective-permute-start.7 = (bf16[1,640,1024]{2,1,0:T(8,128)(2,1)S(1)}, bf16[1,640,1024]{2,1,0:T(8,128)(2,1)S(1)}, u32[]{:S(2)}, u32[]{:S(2)}) collective-permute-start(bf16[1,640,1024]{2,1,0:T(8,128)(2,1)S(1)} %add_convert_fusion.8), channel_id=1, source_target_pairs={{1,0},{2,3},{5,4},{6,7},{9,8},{10,11},{13,12},{14,15},{17,16},{18,... | collective-permute-start | bytes 3932168 | tf_op jit(solution)/shard_map/ppermute | solution.py:228
  249.3 136.0 %collective-permute-start.3 = (bf16[1,640,1024]{2,1,0:T(8,128)(2,1)S(1)}, bf16[1,640,1024]{2,1,0:T(8,128)(2,1)S(1)}, u32[]{:S(2)}, u32[]{:S(2)}) collective-permute-start(bf16[1,640,1024]{2,1,0:T(8,128)(2,1)S(1)} %add_convert_fusion.10), channel_id=1, source_target_pairs={{1,0},{2,3},{5,4},{6,7},{9,8},{10,11},{13,12},{14,15},{17,16},{18,... | collective-permute-start | bytes 3932168 | tf_op jit(solution)/shard_map/ppermute | solution.py:228
  297.5 151.3 %collective-permute-start.28 = (bf16[1,320,1024]{2,1,0:T(8,128)(2,1)}, bf16[1,320,1024]{2,1,0:T(8,128)(2,1)}, u32[]{:S(2)}, u32[]{:S(2)}) collective-permute-start(bf16[1,320,1024]{2,1,0:T(8,128)(2,1)} %get-tuple-element.25), channel_id=1, source_target_pairs={{0,4},{4,0},{1,5},{5,1},{2,6},{6,2},{3,7},{7,3},{8,12},{12,8},{9,1... | collective-permute-start | bytes 1966088 | tf_op jit(solution)/shard_map/ppermute | solution.py:252
  353.9 92.6 %collective-permute-start.26 = (bf16[1,320,1024]{2,1,0:T(8,128)(2,1)}, bf16[1,320,1024]{2,1,0:T(8,128)(2,1)}, u32[]{:S(2)}, u32[]{:S(2)}) collective-permute-start(bf16[1,320,1024]{2,1,0:T(8,128)(2,1)} %get-tuple-element.23), channel_id=1, source_target_pairs={{0,4},{4,0},{1,5},{5,1},{2,6},{6,2},{3,7},{7,3},{8,12},{12,8},{9,1... | collective-permute-start | bytes 1966088 | tf_op jit(solution)/shard_map/ppermute | solution.py:252
  374.0 73.6 %collective-permute-start.27 = (bf16[1,320,1024]{2,1,0:T(8,128)(2,1)}, bf16[1,320,1024]{2,1,0:T(8,128)(2,1)}, u32[]{:S(2)}, u32[]{:S(2)}) collective-permute-start(bf16[1,320,1024]{2,1,0:T(8,128)(2,1)} %get-tuple-element.24), channel_id=1, source_target_pairs={{0,4},{4,0},{1,5},{5,1},{2,6},{6,2},{3,7},{7,3},{8,12},{12,8},{9,1... | collective-permute-start | bytes 1966088 | tf_op jit(solution)/shard_map/ppermute | solution.py:252
  403.0 38.9 %collective-permute-start.24 = (bf16[1,320,1024]{2,1,0:T(8,128)(2,1)S(1)}, bf16[1,320,1024]{2,1,0:T(8,128)(2,1)S(1)}, u32[]{:S(2)}, u32[]{:S(2)}) collective-permute-start(bf16[1,320,1024]{2,1,0:T(8,128)(2,1)S(1)} %get-tuple-element.21), channel_id=1, source_target_pairs={{0,4},{4,0},{1,5},{5,1},{2,6},{6,2},{3,7},{7,3},{8,12},{12,8},{9,1... | collective-permute-start | bytes 1966088 | tf_op jit(solution)/shard_map/ppermute | solution.py:252
  (30 other events, 589.2 us)
